TPU v7x, 32 devices: a whole 2x2x4 slice. The times are simulated.
32 devices in a mesh: seq: 4 (over y, x), fsdp: 8 (over z, core).
Axes of the slice: x: 2, y: 2, z: 4, core: 2. Of those that a mesh axis runs over, the one named last changes fastest.
Arguments:
- layer_in: float32 [2, 4, 1024, 2048], P(None, 'seq', 'fsdp'), may hold values from -6 to 6
- doc_ids: int32 [2, 4, 1024], P(None, 'seq'), may hold values from 0 to 3, as said below
- out_grad: float32 [2, 4, 1024, 2048], P(None, 'seq', 'fsdp'), may hold values from -6 to 6
- query_weight: float32 [2048, 2048], P(('seq', 'fsdp')), may hold values from -0.125 to 0.125
- query_bias: float32 [2048], P(('seq', 'fsdp')), may hold values from -3 to 3
- key_weight: float32 [2048, 2048], P(('seq', 'fsdp')), may hold values from -0.1875 to 0.1875
- value_weight: float32 [2048, 2048], P(('seq', 'fsdp')), may hold values from -0.125 to 0.125
- value_bias: float32 [2048], P(('seq', 'fsdp')), may hold values from -2 to 2
- output_weight: float32 [2048, 2048], P(('seq', 'fsdp')), may hold values from -2 to 2
- output_bias: float32 [2048], P(('seq', 'fsdp')), may hold values from -3 to 3
- first_gain: float32 [2048], P(('seq', 'fsdp')), may hold values from 0.25 to 1.75
- first_shift: float32 [2048], P(('seq', 'fsdp')), may hold values from -2 to 2
- up_weight: float32 [2048, 8192], P(('seq', 'fsdp')), may hold values from -0.125 to 0.125
- up_bias: float32 [8192], P(('seq', 'fsdp')), may hold values from -3 to 3
- down_weight: float32 [8192, 2048], P(('seq', 'fsdp')), may hold values from -0.0625 to 0.0625
- down_bias: float32 [2048], P(('seq', 'fsdp')), may hold values from -3 to 3
- second_gain: float32 [2048], P(('seq', 'fsdp')), may hold values from 0.25 to 1.75
- second_shift: float32 [2048], P(('seq', 'fsdp')), may hold values from -2 to 2
Outputs:
- layer_out: float32 [2, 4, 1024, 2048], P(None, 'seq', 'fsdp')
- input_grad: float32 [2, 4, 1024, 2048], P(None, 'seq', 'fsdp')
- query_weight_grad: float32 [2048, 2048], P(('seq', 'fsdp'))
- query_bias_grad: float32 [2048], P(('seq', 'fsdp'))
- key_weight_grad: float32 [2048, 2048], P(('seq', 'fsdp'))
- value_weight_grad: float32 [2048, 2048], P(('seq', 'fsdp'))
- value_bias_grad: float32 [2048], P(('seq', 'fsdp'))
- output_weight_grad: float32 [2048, 2048], P(('seq', 'fsdp'))
- output_bias_grad: float32 [2048], P(('seq', 'fsdp'))
- first_gain_grad: float32 [2048], P(('seq', 'fsdp'))
- first_shift_grad: float32 [2048], P(('seq', 'fsdp'))
- up_weight_grad: float32 [2048, 8192], P(('seq', 'fsdp'))
- up_bias_grad: float32 [8192], P(('seq', 'fsdp'))
- down_weight_grad: float32 [8192, 2048], P(('seq', 'fsdp'))
- down_bias_grad: float32 [2048], P(('seq', 'fsdp'))
- second_gain_grad: float32 [2048], P(('seq', 'fsdp'))
- second_shift_grad: float32 [2048], P(('seq', 'fsdp'))
Inputs may be any that keep to these rules, and one draw needn't show every extreme that they name: `doc_ids`: within a sequence the document numbers never fall, every one of the 4 numbers occurs, and each document holds 102 to 718 tokens; in every draw some sequence has a document of exactly 718 tokens.
All inputs are finite; a program needn't handle non-finite values.
Results may differ from a plain program's by a relative error of at most 0.015.
The roundings to bfloat16 on the way count: a program that leaves them out, or rounds other values in their place, can miss the bound.
Values may be sent and summed in bfloat16 or wider, within the bound.
No kernel may reach another device: no remote copies, remote signals or barrier semaphores. Data moves between devices by JAX's collectives and lax.ppermute only.
A program may use at most 512 MiB of HBM per device.

v0:
```python
from functools import reduce
import jax
import jax.numpy as jnp
from jax import lax
from jax.sharding import PartitionSpec as P

D = 2048
H = 16
DH = 128
MB = 2
norm_eps = 1e-06
masked_score = -1e30


def normalize_forward(summed, gain_vector, shift_vector):
    center = summed - jnp.mean(summed, axis=-1, keepdims=True)
    inverse = lax.rsqrt(jnp.mean(center * center, axis=-1, keepdims=True) + norm_eps)
    normed = center * inverse
    return (normed * gain_vector + shift_vector, normed, inverse)


def normalize_backward(grad_output, normed, inverse, gain_vector):
    grad_normed = grad_output * gain_vector
    centered = grad_normed - jnp.mean(grad_normed, axis=-1, keepdims=True)
    grad_input = inverse * (
        centered - normed * jnp.mean(grad_normed * normed, axis=-1, keepdims=True)
    )
    return (grad_input, jnp.sum(grad_output * normed, axis=0), jnp.sum(grad_output, axis=0))


def masked_scores(query_heads, key_heads, row_ids, all_ids, score_scale):
    scores = (
        jnp.einsum("thd,shd->hts", query_heads, key_heads, preferred_element_type=jnp.float32)
        * score_scale
    )
    same_doc = row_ids[:, None] == all_ids[None, :]
    return jnp.where(same_doc[None], scores, masked_score)


def matmul(left, right):
    return jnp.dot(left, right, preferred_element_type=jnp.float32)


def transposed(left, right):
    return jnp.einsum("ti,tj->ij", left, right, preferred_element_type=jnp.float32)


def against(left, right):
    return jnp.einsum("ti,ji->tj", left, right, preferred_element_type=jnp.float32)


def gelu_tanh(argument):
    return jax.nn.gelu(argument, approximate=True)


def column_sum(matrix):
    return jnp.sum(matrix.astype(jnp.float32), axis=0)


def weight_terms(factors, norm_terms):
    (
        rounded_in,
        grad_query,
        grad_key,
        grad_value,
        mixed_rows,
        grad_branch,
        hidden_low,
        grad_up,
        active_low,
        grad_down,
    ) = factors
    first_gain_part, first_shift_part, second_gain_part, second_shift_part = norm_terms
    return (
        transposed(rounded_in, grad_query),
        column_sum(grad_query),
        transposed(rounded_in, grad_key),
        transposed(rounded_in, grad_value),
        column_sum(grad_value),
        transposed(mixed_rows, grad_branch),
        column_sum(grad_branch),
        first_gain_part,
        first_shift_part,
        transposed(hidden_low, grad_up),
        column_sum(grad_up),
        transposed(active_low, grad_down),
        column_sum(grad_down),
        second_gain_part,
        second_shift_part,
    )


def shards(
    layer_in,
    doc_ids,
    out_grad,
    query_weight,
    query_bias,
    key_weight,
    value_weight,
    value_bias,
    output_weight,
    output_bias,
    first_gain,
    first_shift,
    up_weight,
    up_bias,
    down_weight,
    down_bias,
    second_gain,
    second_shift,
):
    low_type = jnp.bfloat16
    wide_type = jnp.float32
    local = (
        query_weight.astype(low_type),
        query_bias.astype(low_type),
        key_weight.astype(low_type),
        value_weight.astype(low_type),
        value_bias.astype(low_type),
        output_weight.astype(low_type),
        output_bias.astype(low_type),
        first_gain.astype(low_type),
        first_shift.astype(low_type),
        up_weight.astype(low_type),
        up_bias.astype(low_type),
        down_weight.astype(low_type),
        down_bias.astype(low_type),
        second_gain.astype(low_type),
        second_shift.astype(low_type),
    )
    tokens_here = layer_in.shape[2]
    start_row = lax.axis_index("fsdp") * tokens_here
    score_scale = DH ** (-0.5)
    outputs = []
    input_grads = []
    grad_total = None
    stored_factors = []
    stored_norms = []
    (
        query_matrix,
        query_offset,
        key_matrix,
        value_matrix,
        value_offset,
        output_matrix,
        output_offset,
        first_scale,
        first_offset,
        up_matrix,
        up_offset,
        down_matrix,
        down_offset,
        second_scale,
        second_offset,
    ) = (
        lax.all_gather(local[0], ("seq", "fsdp"), axis=0, tiled=True),
        lax.all_gather(local[1], ("seq", "fsdp"), axis=0, tiled=True),
        lax.all_gather(local[2], ("seq", "fsdp"), axis=0, tiled=True),
        lax.all_gather(local[3], ("seq", "fsdp"), axis=0, tiled=True),
        lax.all_gather(local[4], ("seq", "fsdp"), axis=0, tiled=True),
        lax.all_gather(local[5], ("seq", "fsdp"), axis=0, tiled=True),
        lax.all_gather(local[6], ("seq", "fsdp"), axis=0, tiled=True),
        lax.all_gather(local[7], ("seq", "fsdp"), axis=0, tiled=True),
        lax.all_gather(local[8], ("seq", "fsdp"), axis=0, tiled=True),
        lax.all_gather(local[9], ("seq", "fsdp"), axis=0, tiled=True),
        lax.all_gather(local[10], ("seq", "fsdp"), axis=0, tiled=True),
        lax.all_gather(local[11], ("seq", "fsdp"), axis=0, tiled=True),
        lax.all_gather(local[12], ("seq", "fsdp"), axis=0, tiled=True),
        lax.all_gather(local[13], ("seq", "fsdp"), axis=0, tiled=True),
        lax.all_gather(local[14], ("seq", "fsdp"), axis=0, tiled=True),
    )
    for portion in range(MB):
        inputs = layer_in[portion, 0]
        all_ids = doc_ids[portion, 0]
        row_ids = lax.dynamic_slice_in_dim(all_ids, start_row, tokens_here)
        rounded_in = inputs.astype(low_type)
        query_rows = (matmul(rounded_in, query_matrix) + query_offset.astype(wide_type)).astype(
            low_type
        )
        key_rows = matmul(rounded_in, key_matrix).astype(low_type)
        value_rows = (matmul(rounded_in, value_matrix) + value_offset.astype(wide_type)).astype(
            low_type
        )
        key_whole, value_whole = (
            lax.all_gather(key_rows, "fsdp", axis=0, tiled=True),
            lax.all_gather(value_rows, "fsdp", axis=0, tiled=True),
        )
        length = key_whole.shape[0]
        query_heads = query_rows.reshape(tokens_here, H, DH)
        key_heads = key_whole.reshape(length, H, DH)
        value_heads = value_whole.reshape(length, H, DH)
        scores = masked_scores(query_heads, key_heads, row_ids, all_ids, score_scale)
        row_max = jnp.max(scores, axis=-1, keepdims=True)
        log_total = row_max + jnp.log(jnp.sum(jnp.exp(scores - row_max), axis=-1, keepdims=True))
        attend_low = jnp.exp(scores - log_total).astype(low_type)
        mixed_rows = jnp.einsum(
            "hts,shd->thd", attend_low, value_heads, preferred_element_type=wide_type
        )
        mixed_rows = mixed_rows.reshape(tokens_here, D).astype(low_type)
        branch = matmul(mixed_rows, output_matrix) + output_offset.astype(wide_type)
        hidden, first_normed, first_inverse = normalize_forward(
            inputs + branch, first_scale.astype(wide_type), first_offset.astype(wide_type)
        )
        hidden_low = hidden.astype(low_type)
        up_rows = matmul(hidden_low, up_matrix) + up_offset.astype(wide_type)
        active, gelu_back = jax.vjp(gelu_tanh, up_rows)
        active_low = active.astype(low_type)
        down_rows = matmul(active_low, down_matrix) + down_offset.astype(wide_type)
        result, second_normed, second_inverse = normalize_forward(
            hidden + down_rows, second_scale.astype(wide_type), second_offset.astype(wide_type)
        )
        outputs.append(result)
        (
            query_back,
            key_back,
            value_back,
            output_back,
            first_back,
            up_back,
            down_back,
            second_back,
        ) = (
            query_matrix,
            key_matrix,
            value_matrix,
            output_matrix,
            first_scale,
            up_matrix,
            down_matrix,
            second_scale,
        )
        grad_output = out_grad[portion, 0]
        grad_second, second_gain_part, second_shift_part = normalize_backward(
            grad_output, second_normed, second_inverse, second_back.astype(wide_type)
        )
        grad_down = grad_second.astype(low_type)
        grad_active = against(grad_down, down_back)
        grad_up = gelu_back(grad_active)[0].astype(low_type)
        grad_hidden = grad_second + against(grad_up, up_back)
        grad_first, first_gain_part, first_shift_part = normalize_backward(
            grad_hidden, first_normed, first_inverse, first_back.astype(wide_type)
        )
        grad_branch = grad_first.astype(low_type)
        grad_mixed = against(grad_branch, output_back).astype(low_type)
        grad_heads = grad_mixed.reshape(tokens_here, H, DH)
        scores = masked_scores(query_heads, key_heads, row_ids, all_ids, score_scale)
        attend = jnp.exp(scores - log_total)
        grad_attend = jnp.einsum(
            "thd,shd->hts", grad_heads, value_heads, preferred_element_type=wide_type
        )
        row_dot = jnp.sum(attend * grad_attend, axis=-1, keepdims=True)
        grad_scores = (attend * (grad_attend - row_dot)).astype(low_type)
        grad_query = (
            jnp.einsum("hts,shd->thd", grad_scores, key_heads, preferred_element_type=wide_type)
            * score_scale
        )
        grad_query = grad_query.reshape(tokens_here, D).astype(low_type)
        key_part = (
            jnp.einsum("hts,thd->shd", grad_scores, query_heads, preferred_element_type=wide_type)
            * score_scale
        )
        value_part = jnp.einsum(
            "hts,thd->shd", attend.astype(low_type), grad_heads, preferred_element_type=wide_type
        )
        key_sum, value_sum = (
            lax.psum_scatter(
                key_part.reshape(length, D).astype(jnp.bfloat16),
                "fsdp",
                scatter_dimension=0,
                tiled=True,
            ).astype(jnp.float32),
            lax.psum_scatter(
                value_part.reshape(length, D).astype(jnp.bfloat16),
                "fsdp",
                scatter_dimension=0,
                tiled=True,
            ).astype(jnp.float32),
        )
        grad_key = key_sum.astype(low_type)
        grad_value = value_sum.astype(low_type)
        input_grads.append(
            grad_first
            + against(grad_query, query_back)
            + against(grad_key, key_back)
            + against(grad_value, value_back)
        )
        factors = (
            rounded_in,
            grad_query,
            grad_key,
            grad_value,
            mixed_rows,
            grad_branch,
            hidden_low,
            grad_up,
            active_low,
            grad_down,
        )
        norm_terms = (first_gain_part, first_shift_part, second_gain_part, second_shift_part)
        stored_factors.append(factors)
        stored_norms.append(norm_terms)
    joined = tuple(
        (jnp.concatenate([entry[index] for entry in stored_factors], axis=0) for index in range(10))
    )
    summed_norms = tuple(
        (reduce(jnp.add, [entry[index] for entry in stored_norms]) for index in range(4))
    )
    terms = weight_terms(joined, summed_norms)
    grad_total = (
        lax.psum_scatter(terms[0], ("seq", "fsdp"), scatter_dimension=0, tiled=True),
        lax.psum_scatter(terms[1], ("seq", "fsdp"), scatter_dimension=0, tiled=True),
        lax.psum_scatter(terms[2], ("seq", "fsdp"), scatter_dimension=0, tiled=True),
        lax.psum_scatter(terms[3], ("seq", "fsdp"), scatter_dimension=0, tiled=True),
        lax.psum_scatter(terms[4], ("seq", "fsdp"), scatter_dimension=0, tiled=True),
        lax.psum_scatter(terms[5], ("seq", "fsdp"), scatter_dimension=0, tiled=True),
        lax.psum_scatter(terms[6], ("seq", "fsdp"), scatter_dimension=0, tiled=True),
        lax.psum_scatter(terms[7], ("seq", "fsdp"), scatter_dimension=0, tiled=True),
        lax.psum_scatter(terms[8], ("seq", "fsdp"), scatter_dimension=0, tiled=True),
        lax.psum_scatter(terms[9], ("seq", "fsdp"), scatter_dimension=0, tiled=True),
        lax.psum_scatter(terms[10], ("seq", "fsdp"), scatter_dimension=0, tiled=True),
        lax.psum_scatter(terms[11], ("seq", "fsdp"), scatter_dimension=0, tiled=True),
        lax.psum_scatter(terms[12], ("seq", "fsdp"), scatter_dimension=0, tiled=True),
        lax.psum_scatter(terms[13], ("seq", "fsdp"), scatter_dimension=0, tiled=True),
        lax.psum_scatter(terms[14], ("seq", "fsdp"), scatter_dimension=0, tiled=True),
    )
    layer_out = jnp.stack(outputs)[:, None]
    input_grad = jnp.stack(input_grads)[:, None]
    return (
        layer_out,
        input_grad,
        grad_total[0],
        grad_total[1],
        grad_total[2],
        grad_total[3],
        grad_total[4],
        grad_total[5],
        grad_total[6],
        grad_total[7],
        grad_total[8],
        grad_total[9],
        grad_total[10],
        grad_total[11],
        grad_total[12],
        grad_total[13],
        grad_total[14],
    )


def solution(mesh):
    placed = (
        P(None, "seq", "fsdp", None),
        P(None, "seq", None),
        P(None, "seq", "fsdp", None),
        P(("seq", "fsdp"), None),
        P(("seq", "fsdp")),
        P(("seq", "fsdp"), None),
        P(("seq", "fsdp"), None),
        P(("seq", "fsdp")),
        P(("seq", "fsdp"), None),
        P(("seq", "fsdp")),
        P(("seq", "fsdp")),
        P(("seq", "fsdp")),
        P(("seq", "fsdp"), None),
        P(("seq", "fsdp")),
        P(("seq", "fsdp"), None),
        P(("seq", "fsdp")),
        P(("seq", "fsdp")),
        P(("seq", "fsdp")),
    )
    return jax.shard_map(
        shards,
        mesh=mesh,
        in_specs=placed,
        out_specs=(
            P(None, "seq", "fsdp", None),
            P(None, "seq", "fsdp", None),
            P(("seq", "fsdp"), None),
            P(("seq", "fsdp")),
            P(("seq", "fsdp"), None),
            P(("seq", "fsdp"), None),
            P(("seq", "fsdp")),
            P(("seq", "fsdp"), None),
            P(("seq", "fsdp")),
            P(("seq", "fsdp")),
            P(("seq", "fsdp")),
            P(("seq", "fsdp"), None),
            P(("seq", "fsdp")),
            P(("seq", "fsdp"), None),
            P(("seq", "fsdp")),
            P(("seq", "fsdp")),
            P(("seq", "fsdp")),
        ),
        check_vma=False,
    )
```

profile of v0, /device:TPU:0, one launch (start us, length us, event | category | flops | bytes accessed | tf_op | source)
XLA Modules:
  0.0 3573.6 jit_solution(3197997986055923323)
XLA Ops:
  14.5 77.2 %all-gather.18.cloned.1.call-done = bf16[2048,2048]{1,0:T(8,128)(2,1)} async-done(((bf16[64,2048]{1,0:T(8,128)(2,1)}), bf16[2048,2048]{1,0:T(8,128)(2,1)}) %all-gather.18.cloned.1.call-update) | async-done | bytes 8388624 | tf_op jit(solution)/shard_map/all_gather | solution.py:159
  104.9 40.1 %all-reduce.18 = (bf16[2048]{0:T(1024)(128)(2,1)S(1)}, bf16[2048]{0:T(1024)(128)(2,1)S(1)}, bf16[2048]{0:T(1024)(128)(2,1)S(1)}, bf16[2048]{0:T(1024)(128)(2,1)S...) all-reduce(bf16[2048]{0:T(1024)(128)(2,1)S(1)} %dynamic-update-slic, ...), channel_id=1, replica_groups=mesh['seq'=4,'fsdp'=8] {'seq','fsdp'}, use_global_device_ids=true, to_apply=%add | all-reduce | flops 16384 | bytes 65536
  145.0 26.3 all-gather.12.cloned.1.call-done
  187.3 50.1 %all-gather = bf16[32,1,256]{2,1,0:T(2,128)(2,1)S(1)} all-gather(bf16[1,1,256]{2,1,0:T(2,128)(2,1)S(1)} %reshape.277), channel_id=1, replica_groups=mesh['seq'=4,'fsdp'=8] {'seq','fsdp'}, dimensions={0}, use_global_device_ids=true | all-gather | bytes 16896 | tf_op jit(solution)/shard_map/all_gather | solution.py:167
  262.1 36.9 %all-gather.20.cloned.1.call-done = bf16[1024,2048]{1,0:T(8,128)(2,1)} async-done(((bf16[128,2048]{1,0:T(8,128)(2,1)}), bf16[1024,2048]{1,0:T(8,128)(2,1)}) %all-gather.20.cloned.1.call-update) | async-done | bytes 4194320 | tf_op jit(solution)/shard_map/all_gather | solution.py:186
  305.4 41.5 %all-gather.30.cloned.1.call-done = bf16[1024,2048]{1,0:T(8,128)(2,1)} async-done(((bf16[128,2048]{1,0:T(8,128)(2,1)}), bf16[1024,2048]{1,0:T(8,128)(2,1)}) %all-gather.30.cloned.1.call-update) | async-done | bytes 4194320 | tf_op jit(solution)/shard_map/all_gather | solution.py:186
  360.9 33.9 all-gather.28.cloned.1.call-done
  403.0 71.5 %all-gather.22.cloned.1.call-done = bf16[2048,2048]{1,0:T(8,128)(2,1)} async-done(((bf16[64,2048]{1,0:T(8,128)(2,1)}), bf16[2048,2048]{1,0:T(8,128)(2,1)}) %all-gather.22.cloned.1.call-update) | async-done | bytes 8388624 | tf_op jit(solution)/shard_map/all_gather | solution.py:162
  485.2 37.3 %all-gather.14.cloned.1.call-done = bf16[1024,2048]{1,0:T(8,128)(2,1)} async-done(((bf16[128,2048]{1,0:T(8,128)(2,1)}), bf16[1024,2048]{1,0:T(8,128)(2,1)}) %all-gather.14.cloned.1.call-update) | async-done | bytes 4194320 | tf_op jit(solution)/shard_map/all_gather | solution.py:187
  536.3 183.4 %all-gather.24.cloned.1.call-done = bf16[2048,8192]{1,0:T(8,128)(2,1)} async-done(((bf16[64,8192]{1,0:T(8,128)(2,1)}), bf16[2048,8192]{1,0:T(8,128)(2,1)}) %all-gather.24.cloned.1.call-update) | async-done | bytes 33554448 | tf_op jit(solution)/shard_map/all_gather | solution.py:166
  736.4 179.6 %all-gather.26.cloned.1.call-done = bf16[8192,2048]{1,0:T(8,128)(2,1)} async-done(((bf16[256,2048]{1,0:T(8,128)(2,1)}), bf16[8192,2048]{1,0:T(8,128)(2,1)}) %all-gather.26.cloned.1.call-update) | async-done | bytes 33554448 | tf_op jit(solution)/shard_map/all_gather | solution.py:168
  983.6 19.7 multiply_reduce_fusion.3
  1022.1 19.9 fusion.90
  1188.9 26.6 reduce-scatter.35.cloned.1.call-done
  1217.6 48.3 %reduce-scatter.31.cloned.1.call-done = bf16[128,2048]{1,0:T(8,128)(2,1)} async-done(((bf16[1024,2048]{1,0:T(8,128)(2,1)}), bf16[128,2048]{1,0:T(8,128)(2,1)}) %reduce-scatter.31.cloned.1.call-update) | async-done | bytes 524304
  1287.8 24.9 fusion.34
  1314.5 25.0 fusion.26
  1368.8 26.5 all-reduce.21.cloned.1.call-done
  1406.7 179.1 %reduce-scatter.19.cloned.1.call-done = f32[64,2048]{1,0:T(8,128)} async-done(((f32[2048,2048]{1,0:T(8,128)}), f32[64,2048]{1,0:T(8,128)}) %reduce-scatter.19.cloned.1.call-update) | async-done | bytes 524304 | tf_op jit(solution)/shard_map/reduce_scatter | solution.py:311
  1585.8 187.2 %reduce-scatter.25.cloned.1.call-done = f32[64,2048]{1,0:T(8,128)} async-done(((f32[2048,2048]{1,0:T(8,128)}), f32[64,2048]{1,0:T(8,128)}) %reduce-scatter.25.cloned.1.call-update) | async-done | bytes 524304 | tf_op jit(solution)/shard_map/reduce_scatter | solution.py:316
  1773.0 187.2 %reduce-scatter.21.cloned.1.call-done = f32[64,2048]{1,0:T(8,128)} async-done(((f32[2048,2048]{1,0:T(8,128)}), f32[64,2048]{1,0:T(8,128)}) %reduce-scatter.21.cloned.1.call-update) | async-done | bytes 524304 | tf_op jit(solution)/shard_map/reduce_scatter | solution.py:313
  1960.2 187.3 %reduce-scatter.23.cloned.1.call-done = f32[64,2048]{1,0:T(8,128)} async-done(((f32[2048,2048]{1,0:T(8,128)}), f32[64,2048]{1,0:T(8,128)}) %reduce-scatter.23.cloned.1.call-update) | async-done | bytes 524304 | tf_op jit(solution)/shard_map/reduce_scatter | solution.py:314
  2147.6 710.0 %reduce-scatter.27.cloned.1.call-done = f32[64,8192]{1,0:T(8,128)} async-done(((f32[2048,8192]{1,0:T(8,128)}), f32[64,8192]{1,0:T(8,128)}) %reduce-scatter.27.cloned.1.call-update) | async-done | bytes 2097168 | tf_op jit(solution)/shard_map/reduce_scatter | solution.py:320
  2857.6 709.0 %reduce-scatter.29.cloned.1.call-done = f32[256,2048]{1,0:T(8,128)} async-done(((f32[8192,2048]{1,0:T(8,128)}), f32[256,2048]{1,0:T(8,128)}) %reduce-scatter.29.cloned.1.call-update) | async-done | bytes 2097168 | tf_op jit(solution)/shard_map/reduce_scatter | solution.py:322
  (322 shorter events, 429.3 us)
Async XLA Ops:
  7.2 84.5 %all-gather.18.cloned.1.call-start = ((), (), s32[]{:S(2)}) async-start(), calls=%async_computation.13 | async-start | bytes 8650752 | tf_op jit(solution)/shard_map/all_gather | solution.py:159
  9.0 162.3 %all-gather.12.cloned.1.call-start = ((), (), s32[]{:S(2)}) async-start(), calls=%async_computation.10 | async-start | bytes 8650752 | tf_op jit(solution)/shard_map/all_gather | solution.py:160
  10.9 240.3 %all-gather.16.cloned.1.call-start = ((), (), s32[]{:S(2)}) async-start(), calls=%async_computation.12 | async-start | bytes 8650752 | tf_op jit(solution)/shard_map/all_gather | solution.py:157
  12.7 286.2 %all-gather.20.cloned.1.call-start = ((), (), s32[]{:S(2)}) async-start(), calls=%async_computation.14 | async-start | bytes 4718592 | tf_op jit(solution)/shard_map/all_gather | solution.py:186
  14.5 236.7 %copy-start.2 = (bf16[128,2048]{1,0:T(8,128)(2,1)}, bf16[128,2048]{1,0:T(8,128)(2,1)S(1)}, u32[]{:S(2)}) copy-start(bf16[128,2048]{1,0:T(8,128)(2,1)S(1)} %get-tuple-element.96) | copy-start | bytes 1572868
  14.5 242.3 %copy-start.4 = (bf16[128,2048]{1,0:T(8,128)(2,1)}, bf16[128,2048]{1,0:T(8,128)(2,1)S(1)}, u32[]{:S(2)}) copy-start(bf16[128,2048]{1,0:T(8,128)(2,1)S(1)} %get-tuple-element.97) | copy-start | bytes 1572868
  97.2 249.7 %all-gather.30.cloned.1.call-start = ((), (), s32[]{:S(2)}) async-start(), calls=%async_computation.19 | async-start | bytes 4718592 | tf_op jit(solution)/shard_map/all_gather | solution.py:186
  102.8 292.0 %all-gather.28.cloned.1.call-start = ((), (), s32[]{:S(2)}) async-start(), calls=%async_computation.18 | async-start | bytes 4718592 | tf_op jit(solution)/shard_map/all_gather | solution.py:187
  176.8 297.7 %all-gather.22.cloned.1.call-start = ((), (), s32[]{:S(2)}) async-start(), calls=%async_computation.15 | async-start | bytes 8650752 | tf_op jit(solution)/shard_map/all_gather | solution.py:162
  177.6 344.9 %all-gather.14.cloned.1.call-start = ((), (), s32[]{:S(2)}) async-start(), calls=%async_computation.11 | async-start | bytes 4718592 | tf_op jit(solution)/shard_map/all_gather | solution.py:187
  183.3 536.4 %all-gather.24.cloned.1.call-start = ((), (), s32[]{:S(2)}) async-start(), calls=%async_computation.16 | async-start | bytes 34603008 | tf_op jit(solution)/shard_map/all_gather | solution.py:166
  184.4 731.6 %all-gather.26.cloned.1.call-start = ((), (), s32[]{:S(2)}) async-start(), calls=%async_computation.17 | async-start | bytes 34603008 | tf_op jit(solution)/shard_map/all_gather | solution.py:168
  187.2 963.6 %reduce-scatter.37.cloned.1.call-start = ((), (), s32[]{:S(2)}) async-start(), calls=%async_computation.29 | async-start | bytes 4718592
  536.2 393.7 %copy-start.41 = (bf16[128,2048]{1,0:T(8,128)(2,1)}, bf16[128,2048]{1,0:T(8,128)(2,1)S(1)}, u32[]{:S(2)}) copy-start(bf16[128,2048]{1,0:T(8,128)(2,1)S(1)} %get-tuple-element.101) | copy-start | bytes 1572868
  1066.4 98.7 %reduce-scatter.33.cloned.1.call-start = ((), (), s32[]{:S(2)}) async-start(), calls=%async_computation.27 | async-start | bytes 4718592
  1087.7 127.8 %reduce-scatter.35.cloned.1.call-start = ((), (), s32[]{:S(2)}) async-start(), calls=%async_computation.28 | async-start | bytes 4718592
  1111.3 154.6 %reduce-scatter.31.cloned.1.call-start = ((), (), s32[]{:S(2)}) async-start(), calls=%async_computation.26 | async-start | bytes 4718592
  1134.8 260.5 %all-reduce.21.cloned.1.call-start = ((), (), s32[]{:S(2)}) async-start(), calls=%async_computation.30 | async-start | bytes 196608
  1169.3 416.5 %reduce-scatter.19.cloned.1.call-start = ((), (), s32[]{:S(2)}) async-start(), calls=%async_computation.20 | async-start | bytes 17301504 | tf_op jit(solution)/shard_map/reduce_scatter | solution.py:311
  1179.1 593.9 %reduce-scatter.25.cloned.1.call-start = ((), (), s32[]{:S(2)}) async-start(), calls=%async_computation.23 | async-start | bytes 17301504 | tf_op jit(solution)/shard_map/reduce_scatter | solution.py:316
  1188.8 771.4 %reduce-scatter.21.cloned.1.call-start = ((), (), s32[]{:S(2)}) async-start(), calls=%async_computation.21 | async-start | bytes 17301504 | tf_op jit(solution)/shard_map/reduce_scatter | solution.py:313
  1277.3 870.3 %reduce-scatter.23.cloned.1.call-start = ((), (), s32[]{:S(2)}) async-start(), calls=%async_computation.22 | async-start | bytes 17301504 | tf_op jit(solution)/shard_map/reduce_scatter | solution.py:314
  1286.7 1570.9 %reduce-scatter.27.cloned.1.call-start = ((), (), s32[]{:S(2)}) async-start(), calls=%async_computation.24 | async-start | bytes 69206016 | tf_op jit(solution)/shard_map/reduce_scatter | solution.py:320
  1312.7 2253.9 %reduce-scatter.29.cloned.1.call-start = ((), (), s32[]{:S(2)}) async-start(), calls=%async_computation.25 | async-start | bytes 69206016 | tf_op jit(solution)/shard_map/reduce_scatter | solution.py:322
  (60 other events, 1012.5 us)
Sparse Core Ops, SparseCore 0:
  11.6 80.0 all-gather.17
  95.3 76.0 all-gather.11
  174.9 76.2 all-gather.15
  253.2 45.7 all-gather.19
  301.0 45.8 all-gather.29
  348.9 45.8 all-gather.27
  398.4 76.1 all-gather.21
  476.7 45.7 all-gather.13
  526.0 193.5 all-gather.23
  723.0 192.9 all-gather.25
  1066.5 48.1 reduce-scatter.36
  1116.9 48.1 reduce-scatter.32
  1167.4 48.1 reduce-scatter.34
  1217.7 48.1 reduce-scatter.30
  1272.1 123.1 all-reduce.20
  1398.1 187.6 reduce-scatter.18
  1588.6 184.3 reduce-scatter.24
  1775.8 184.3 reduce-scatter.20
  1963.2 184.3 reduce-scatter.22
  2150.5 707.0 reduce-scatter.26
  2860.6 705.9 reduce-scatter.28
where the time goes:
time: 3580 us; the launch traced here: 3570 us
  waiting for transfers between devices  2970 us (83%)
  matrix products  372 us (10%)
  blocking collectives  90.2 us (3%)
  local copies, waits for them, and re-layouts  73.9 us (2%)
  other arithmetic  45.7 us (1%)
    reduce_scatter x1, waiting for transfers between devices, shards(): lax.psum_scatter(terms[9], ('seq', 'fsdp'), scatter_dimension=0, tiled=True)  710 us
    reduce_scatter x1, waiting for transfers between devices, shards(): lax.psum_scatter(terms[11], ('seq', 'fsdp'), scatter_dimension=0, tiled=T...  709 us
    reduce_scatter x1, waiting for transfers between devices, shards(): lax.psum_scatter(terms[3], ('seq', 'fsdp'), scatter_dimension=0, tiled=True)  187 us
    reduce_scatter x1, waiting for transfers between devices, shards(): lax.psum_scatter(terms[2], ('seq', 'fsdp'), scatter_dimension=0, tiled=True)  187 us
    reduce_scatter x1, waiting for transfers between devices, shards(): lax.psum_scatter(terms[5], ('seq', 'fsdp'), scatter_dimension=0, tiled=True)  187 us
    all_gather x1, waiting for transfers between devices, shards(): lax.all_gather(local[9], ('seq', 'fsdp'), axis=0, tiled=True)  183 us
    all_gather x1, waiting for transfers between devices, shards(): lax.all_gather(local[11], ('seq', 'fsdp'), axis=0, tiled=True)  180 us
    reduce_scatter x1, waiting for transfers between devices, shards(): lax.psum_scatter(terms[0], ('seq', 'fsdp'), scatter_dimension=0, tiled=True)  179 us
  transfers between devices with their start and end apart: 21, of which 20 were waited for; matrix products, arithmetic and copies ran while one was open for 9% of the time, Pallas kernels for 0%

commit v1 on v0

--- a/solution.py
+++ b/solution.py
@@ -10,6 +10,27 @@
 MB = 2
 norm_eps = 1e-06
 masked_score = -1e30
+
+
+def collect(x, axis, dim):
+    size, mine, extent = (lax.axis_size(axis), lax.axis_index(axis), x.shape[dim])
+    right = [(i, (i + 1) % size) for i in range(size)]
+    left = [(i, (i - 1) % size) for i in range(size)]
+    whole = jnp.zeros((*x.shape[:dim], size * extent, *x.shape[dim + 1 :]), x.dtype)
+    whole = lax.dynamic_update_slice_in_dim(whole, x, mine * extent, axis=dim)
+    from_left = from_right = x
+    middle = size // 2
+    for step in range(1, middle + 1):
+        from_left = lax.ppermute(from_left, axis, right)
+        whole = lax.dynamic_update_slice_in_dim(
+            whole, from_left, (mine - step) % size * extent, axis=dim
+        )
+        if step < size - middle:
+            from_right = lax.ppermute(from_right, axis, left)
+            whole = lax.dynamic_update_slice_in_dim(
+                whole, from_right, (mine + step) % size * extent, axis=dim
+            )
+    return whole
 
 
 def normalize_forward(summed, gain_vector, shift_vector):
@@ -183,7 +204,7 @@
             low_type
         )
         key_whole, value_whole = (
-            lax.all_gather(key_rows, "fsdp", axis=0, tiled=True),
+            collect(key_rows, "fsdp", 0),
             lax.all_gather(value_rows, "fsdp", axis=0, tiled=True),
         )
         length = key_whole.shape[0]

time: 3580 us -> 3520 us (0.983)
  waiting for transfers between devices: 2970 us -> 2880 us
    all_gather x2 -> x0, waiting for transfers between devices: 78.4 us -> none  [shards(): lax.all_gather(key_rows, 'fsdp', axis=0, tiled=True)]
    ppermute x0 -> x14, waiting for transfers between devices: none -> 61.9 us  [the longest x8 51.9 us: collect(): from_left = lax.ppermute(from_left, axis, right)]
    all_gather x1, waiting for transfers between devices: 13.3 us -> 69.1 us  [shards(): lax.all_gather(local[0], ('seq', 'fsdp'), axis=0, tiled=True)]
    all_gather x1, waiting for transfers between devices: 77.2 us -> 23.5 us  [shards(): lax.all_gather(local[2], ('seq', 'fsdp'), axis=0, tiled=True)]
    all_gather x1, waiting for transfers between devices: 71.5 us -> 18.7 us  [shards(): lax.all_gather(local[5], ('seq', 'fsdp'), axis=0, tiled=True)]
    unnamed x26 -> x24, waiting for transfers between devices: 114 us -> 113 us
  transfers between devices with their start and end apart: 21 -> 33, of which waited for: 20 -> 23; matrix products, arithmetic and copies ran while one was open for 9% -> 10% of each run, Pallas kernels for 0% -> 0%
where the time goes in v1:
time: 3520 us; the launch traced here: 3510 us
  waiting for transfers between devices  2880 us (82%)
  matrix products  367 us (10%)
  local copies, waits for them, and re-layouts  95.4 us (3%)
  blocking collectives  82.3 us (2%)
  other arithmetic  51.2 us (1%)
    reduce_scatter x1, waiting for transfers between devices, shards(): lax.psum_scatter(terms[9], ('seq', 'fsdp'), scatter_dimension=0, tiled=True)  710 us
    reduce_scatter x1, waiting for transfers between devices, shards(): lax.psum_scatter(terms[11], ('seq', 'fsdp'), scatter_dimension=0, tiled=T...  709 us
    reduce_scatter x1, waiting for transfers between devices, shards(): lax.psum_scatter(terms[2], ('seq', 'fsdp'), scatter_dimension=0, tiled=True)  187 us
    reduce_scatter x1, waiting for transfers between devices, shards(): lax.psum_scatter(terms[3], ('seq', 'fsdp'), scatter_dimension=0, tiled=True)  187 us
    reduce_scatter x1, waiting for transfers between devices, shards(): lax.psum_scatter(terms[5], ('seq', 'fsdp'), scatter_dimension=0, tiled=True)  187 us
    all_gather x1, waiting for transfers between devices, shards(): lax.all_gather(local[9], ('seq', 'fsdp'), axis=0, tiled=True)  183 us
    all_gather x1, waiting for transfers between devices, shards(): lax.all_gather(local[11], ('seq', 'fsdp'), axis=0, tiled=True)  180 us
    reduce_scatter x1, waiting for transfers between devices, shards(): lax.psum_scatter(terms[0], ('seq', 'fsdp'), scatter_dimension=0, tiled=True)  179 us
  transfers between devices with their start and end apart: 33, of which 23 were waited for; matrix products, arithmetic and copies ran while one was open for 10% of the time, Pallas kernels for 0%

profile of v1, /device:TPU:0, one launch (start us, length us, event | category | flops | bytes accessed | tf_op | source)
XLA Modules:
  0.0 3507.8 jit_solution(1484723465264510951)
XLA Ops:
  19.8 42.9 %all-reduce.18 = (bf16[2048]{0:T(1024)(128)(2,1)S(1)}, bf16[2048]{0:T(1024)(128)(2,1)S(1)}, bf16[2048]{0:T(1024)(128)(2,1)S(1)}, bf16[2048]{0:T(1024)(128)(2,1)S...) all-reduce(bf16[2048]{0:T(1024)(128)(2,1)S(1)} %dynamic-update-slic, ...), channel_id=1, replica_groups=mesh['seq'=4,'fsdp'=8] {'seq','fsdp'}, use_global_device_ids=true, to_apply=%add | all-reduce | flops 16384 | bytes 65536
  64.4 27.4 all-gather.10.cloned.1.call-done
  108.0 39.4 %all-gather = bf16[32,1,256]{2,1,0:T(2,128)(2,1)S(1)} all-gather(bf16[1,1,256]{2,1,0:T(2,128)(2,1)S(1)} %reshape.277), channel_id=1, replica_groups=mesh['seq'=4,'fsdp'=8] {'seq','fsdp'}, dimensions={0}, use_global_device_ids=true | all-gather | bytes 16896 | tf_op jit(solution)/shard_map/all_gather | solution.py:188
  148.0 23.5 all-gather.16.cloned.1.call-done
  185.3 69.1 %all-gather.14.cloned.1.call-done = bf16[2048,2048]{1,0:T(8,128)(2,1)} async-done(((bf16[64,2048]{1,0:T(8,128)(2,1)}), bf16[2048,2048]{1,0:T(8,128)(2,1)}) %all-gather.14.cloned.1.call-update) | async-done | bytes 8388624 | tf_op jit(solution)/shard_map/all_gather | solution.py:178
  297.9 21.1 collective-permute-done.2
  414.2 42.6 %all-gather.24.cloned.1.call-done = bf16[1024,2048]{1,0:T(8,128)(2,1)} async-done(((bf16[128,2048]{1,0:T(8,128)(2,1)}), bf16[1024,2048]{1,0:T(8,128)(2,1)}) %all-gather.24.cloned.1.call-update) | async-done | bytes 4194320 | tf_op jit(solution)/shard_map/all_gather | solution.py:208
  470.6 183.3 %all-gather.20.cloned.1.call-done = bf16[2048,8192]{1,0:T(8,128)(2,1)} async-done(((bf16[64,8192]{1,0:T(8,128)(2,1)}), bf16[2048,8192]{1,0:T(8,128)(2,1)}) %all-gather.20.cloned.1.call-update) | async-done | bytes 33554448 | tf_op jit(solution)/shard_map/all_gather | solution.py:187
  670.9 179.6 %all-gather.22.cloned.1.call-done = bf16[8192,2048]{1,0:T(8,128)(2,1)} async-done(((bf16[256,2048]{1,0:T(8,128)(2,1)}), bf16[8192,2048]{1,0:T(8,128)(2,1)}) %all-gather.22.cloned.1.call-update) | async-done | bytes 33554448 | tf_op jit(solution)/shard_map/all_gather | solution.py:189
  898.7 19.2 fusion.10
  917.9 19.5 multiply_reduce_fusion.3
  937.4 18.8 fusion.17
  956.2 20.1 fusion.92
  1122.9 26.9 reduce-scatter.35.cloned.1.call-done
  1151.8 48.3 %reduce-scatter.31.cloned.1.call-done = bf16[128,2048]{1,0:T(8,128)(2,1)} async-done(((bf16[1024,2048]{1,0:T(8,128)(2,1)}), bf16[128,2048]{1,0:T(8,128)(2,1)}) %reduce-scatter.31.cloned.1.call-update) | async-done | bytes 524304
  1222.1 24.9 fusion.34
  1248.8 25.1 fusion.26
  1303.1 26.6 all-reduce.21.cloned.1.call-done
  1341.1 179.1 %reduce-scatter.19.cloned.1.call-done = f32[64,2048]{1,0:T(8,128)} async-done(((f32[2048,2048]{1,0:T(8,128)}), f32[64,2048]{1,0:T(8,128)}) %reduce-scatter.19.cloned.1.call-update) | async-done | bytes 524304 | tf_op jit(solution)/shard_map/reduce_scatter | solution.py:332
  1520.2 187.2 %reduce-scatter.25.cloned.1.call-done = f32[64,2048]{1,0:T(8,128)} async-done(((f32[2048,2048]{1,0:T(8,128)}), f32[64,2048]{1,0:T(8,128)}) %reduce-scatter.25.cloned.1.call-update) | async-done | bytes 524304 | tf_op jit(solution)/shard_map/reduce_scatter | solution.py:337
  1707.4 187.2 %reduce-scatter.21.cloned.1.call-done = f32[64,2048]{1,0:T(8,128)} async-done(((f32[2048,2048]{1,0:T(8,128)}), f32[64,2048]{1,0:T(8,128)}) %reduce-scatter.21.cloned.1.call-update) | async-done | bytes 524304 | tf_op jit(solution)/shard_map/reduce_scatter | solution.py:334
  1894.7 187.2 %reduce-scatter.23.cloned.1.call-done = f32[64,2048]{1,0:T(8,128)} async-done(((f32[2048,2048]{1,0:T(8,128)}), f32[64,2048]{1,0:T(8,128)}) %reduce-scatter.23.cloned.1.call-update) | async-done | bytes 524304 | tf_op jit(solution)/shard_map/reduce_scatter | solution.py:335
  2081.9 710.0 %reduce-scatter.27.cloned.1.call-done = f32[64,8192]{1,0:T(8,128)} async-done(((f32[2048,8192]{1,0:T(8,128)}), f32[64,8192]{1,0:T(8,128)}) %reduce-scatter.27.cloned.1.call-update) | async-done | bytes 2097168 | tf_op jit(solution)/shard_map/reduce_scatter | solution.py:341
  2791.9 709.0 %reduce-scatter.29.cloned.1.call-done = f32[256,2048]{1,0:T(8,128)} async-done(((f32[8192,2048]{1,0:T(8,128)}), f32[256,2048]{1,0:T(8,128)}) %reduce-scatter.29.cloned.1.call-update) | async-done | bytes 2097168 | tf_op jit(solution)/shard_map/reduce_scatter | solution.py:343
  (360 shorter events, 474.1 us)
Async XLA Ops:
  7.2 84.7 %all-gather.10.cloned.1.call-start = ((), (), s32[]{:S(2)}) async-start(), calls=%async_computation.10 | async-start | bytes 8650752 | tf_op jit(solution)/shard_map/all_gather | solution.py:181
  9.0 162.4 %all-gather.16.cloned.1.call-start = ((), (), s32[]{:S(2)}) async-start(), calls=%async_computation.13 | async-start | bytes 8650752 | tf_op jit(solution)/shard_map/all_gather | solution.py:180
  10.9 243.4 %all-gather.14.cloned.1.call-start = ((), (), s32[]{:S(2)}) async-start(), calls=%async_computation.12 | async-start | bytes 8650752 | tf_op jit(solution)/shard_map/all_gather | solution.py:178
  12.7 369.9 %all-gather.12.cloned.1.call-start = ((), (), s32[]{:S(2)}) async-start(), calls=%async_computation.11 | async-start | bytes 4718592 | tf_op jit(solution)/shard_map/all_gather | solution.py:208
  97.4 311.6 %all-gather.18.cloned.1.call-start = ((), (), s32[]{:S(2)}) async-start(), calls=%async_computation.14 | async-start | bytes 8650752 | tf_op jit(solution)/shard_map/all_gather | solution.py:183
  98.2 358.6 %all-gather.24.cloned.1.call-start = ((), (), s32[]{:S(2)}) async-start(), calls=%async_computation.17 | async-start | bytes 4718592 | tf_op jit(solution)/shard_map/all_gather | solution.py:208
  103.9 550.0 %all-gather.20.cloned.1.call-start = ((), (), s32[]{:S(2)}) async-start(), calls=%async_computation.15 | async-start | bytes 34603008 | tf_op jit(solution)/shard_map/all_gather | solution.py:187
  105.0 745.4 %all-gather.22.cloned.1.call-start = ((), (), s32[]{:S(2)}) async-start(), calls=%async_computation.16 | async-start | bytes 34603008 | tf_op jit(solution)/shard_map/all_gather | solution.py:189
  107.8 978.4 %reduce-scatter.37.cloned.1.call-start = ((), (), s32[]{:S(2)}) async-start(), calls=%async_computation.27 | async-start | bytes 4718592
  176.3 92.9 %collective-permute-start.7 = (bf16[128,2048]{1,0:T(8,128)(2,1)S(1)}, bf16[128,2048]{1,0:T(8,128)(2,1)}, u32[]{:S(2)}, u32[]{:S(2)}) collective-permute-start(bf16[128,2048]{1,0:T(8,128)(2,1)S(1)} %convolution_convert_fusion.4), channel_id=1, source_target_pairs={{0,1},{1,2},{2,3},{3,4},{4,5},{5,6},{6,7},{7,0},{8,9},{9,10},{10,1... | collective-permute-start | bytes 1572872 | tf_op jit(solution)/shard_map/ppermute | solution.py:24
  176.6 98.9 %collective-permute-start.8 = (bf16[128,2048]{1,0:T(8,128)(2,1)S(1)}, bf16[128,2048]{1,0:T(8,128)(2,1)}, u32[]{:S(2)}, u32[]{:S(2)}) collective-permute-start(bf16[128,2048]{1,0:T(8,128)(2,1)S(1)} %convolution_convert_fusion.4), channel_id=1, source_target_pairs={{0,7},{1,0},{2,1},{3,2},{4,3},{5,4},{6,5},{7,6},{8,15},{9,8},{10,9... | collective-permute-start | bytes 1572872 | tf_op jit(solution)/shard_map/ppermute | solution.py:29
  181.5 89.5 %collective-permute-start = (bf16[128,2048]{1,0:T(8,128)(2,1)S(1)}, bf16[128,2048]{1,0:T(8,128)(2,1)}, u32[]{:S(2)}, u32[]{:S(2)}) collective-permute-start(bf16[128,2048]{1,0:T(8,128)(2,1)S(1)} %convolution_convert_fusion.5), channel_id=1, source_target_pairs={{0,1},{1,2},{2,3},{3,4},{4,5},{5,6},{6,7},{7,0},{8,9},{9,10},{10,1... | collective-permute-start | bytes 1572872 | tf_op jit(solution)/shard_map/ppermute | solution.py:24
  181.5 97.6 %collective-permute-start.1 = (bf16[128,2048]{1,0:T(8,128)(2,1)S(1)}, bf16[128,2048]{1,0:T(8,128)(2,1)}, u32[]{:S(2)}, u32[]{:S(2)}) collective-permute-start(bf16[128,2048]{1,0:T(8,128)(2,1)S(1)} %convolution_convert_fusion.5), channel_id=1, source_target_pairs={{0,7},{1,0},{2,1},{3,2},{4,3},{5,4},{6,5},{7,6},{8,15},{9,8},{10,9... | collective-permute-start | bytes 1572872 | tf_op jit(solution)/shard_map/ppermute | solution.py:29
  272.3 46.7 %collective-permute-start.2 = (bf16[128,2048]{1,0:T(8,128)(2,1)}, bf16[128,2048]{1,0:T(8,128)(2,1)}, u32[]{:S(2)}, u32[]{:S(2)}) collective-permute-start(bf16[128,2048]{1,0:T(8,128)(2,1)} %collective-permute-done), channel_id=1, source_target_pairs={{0,1},{1,2},{2,3},{3,4},{4,5},{5,6},{6,7},{7,0},{8,9},{9,10},{10,1... | collective-permute-start | bytes 1572872 | tf_op jit(solution)/shard_map/ppermute | solution.py:24
  1000.7 98.7 %reduce-scatter.33.cloned.1.call-start = ((), (), s32[]{:S(2)}) async-start(), calls=%async_computation.25 | async-start | bytes 4718592
  1022.0 127.8 %reduce-scatter.35.cloned.1.call-start = ((), (), s32[]{:S(2)}) async-start(), calls=%async_computation.26 | async-start | bytes 4718592
  1045.1 155.0 %reduce-scatter.31.cloned.1.call-start = ((), (), s32[]{:S(2)}) async-start(), calls=%async_computation.24 | async-start | bytes 4718592
  1068.9 260.8 %all-reduce.21.cloned.1.call-start = ((), (), s32[]{:S(2)}) async-start(), calls=%async_computation.28 | async-start | bytes 196608
  1103.5 416.7 %reduce-scatter.19.cloned.1.call-start = ((), (), s32[]{:S(2)}) async-start(), calls=%async_computation.18 | async-start | bytes 17301504 | tf_op jit(solution)/shard_map/reduce_scatter | solution.py:332
  1113.1 594.3 %reduce-scatter.25.cloned.1.call-start = ((), (), s32[]{:S(2)}) async-start(), calls=%async_computation.21 | async-start | bytes 17301504 | tf_op jit(solution)/shard_map/reduce_scatter | solution.py:337
  1122.9 771.8 %reduce-scatter.21.cloned.1.call-start = ((), (), s32[]{:S(2)}) async-start(), calls=%async_computation.19 | async-start | bytes 17301504 | tf_op jit(solution)/shard_map/reduce_scatter | solution.py:334
  1211.5 870.4 %reduce-scatter.23.cloned.1.call-start = ((), (), s32[]{:S(2)}) async-start(), calls=%async_computation.20 | async-start | bytes 17301504 | tf_op jit(solution)/shard_map/reduce_scatter | solution.py:335
  1220.9 1571.0 %reduce-scatter.27.cloned.1.call-start = ((), (), s32[]{:S(2)}) async-start(), calls=%async_computation.22 | async-start | bytes 69206016 | tf_op jit(solution)/shard_map/reduce_scatter | solution.py:341
  1247.0 2253.9 %reduce-scatter.29.cloned.1.call-start = ((), (), s32[]{:S(2)}) async-start(), calls=%async_computation.23 | async-start | bytes 69206016 | tf_op jit(solution)/shard_map/reduce_scatter | solution.py:343
  (64 other events, 2005.9 us)
Sparse Core Ops, SparseCore 0:
  11.6 80.2 all-gather.9
  95.4 76.0 all-gather.15
  175.0 79.2 all-gather.13
  256.3 62.4 all-gather.11
  322.3 86.6 all-gather.17
  411.0 45.7 all-gather.23
  460.4 193.4 all-gather.19
  657.5 192.9 all-gather.21
  1000.8 48.1 reduce-scatter.36
  1051.1 48.1 reduce-scatter.32
  1101.6 48.1 reduce-scatter.34
  1151.9 48.1 reduce-scatter.30
  1206.5 123.1 all-reduce.20
  1332.5 187.6 reduce-scatter.18
  1523.0 184.3 reduce-scatter.24
  1710.3 184.3 reduce-scatter.20
  1897.5 184.3 reduce-scatter.22
  2084.8 707.0 reduce-scatter.26
  2795.0 705.9 reduce-scatter.28
